TPU v7x, 256 devices: a whole 4x4x8 slice. The times are simulated.
256 devices in a mesh: op: 32 (over x, z_hi, core), sec: 8 (over y, z_lo).
Axes of the slice: x: 4, y: 4, z: 8 (z_hi: 4, z_lo: 2; z = z_hi * 2 + z_lo), core: 2. Of those that a mesh axis runs over, the one named last changes fastest.
Arguments:
- left_ops: float32 [32, 8, 1024, 1024], P('op', 'sec'), may hold values from -0.5 to 3.5
- right_ops: float32 [32, 8, 1024, 1024], P('op', 'sec'), may hold values from -0.5 to 3.5
- amplitudes: float32 [8, 1024, 1024], P('sec', 'op'), may hold values from -72 to 72
- sketch: float32 [1024, 512], replicated, may hold values from -0.1875 to 0.1875
- sector_shift: int32 [32], P('op'), may hold values from 0 to 3
Outputs:
- rotated: float32 [32, 8, 512, 512], P('op', 'sec')
- new_basis: float32 [8, 1024, 512], P('sec', 'op')
- energy: float32 [], replicated
Inputs may be any that keep to these rules, and one draw needn't show every extreme that they name: The target sector of pair k from source sector s is (s + sector_shift[k]) mod 8.
All inputs are finite; a program needn't handle non-finite values.
Results may differ from a plain program's by a relative error of at most 0.0003.
Values sent between devices are 32-bit elements; how exact they have to be, the bound alone decides.
No kernel may reach another device: no remote copies, remote signals or barrier semaphores. Data moves between devices by JAX's collectives and lax.ppermute only.
A program may use at most 128 MiB of HBM per device.

v0:
```python
import jax
import jax.numpy as jnp
from jax import lax
from jax.sharding import Mesh
from jax.sharding import PartitionSpec as P

OP = ("op_0", "op_1", "op_2")
SEC = ("sec_0", "sec_1")
OP_SEC = ("op_0", "op_1", "op_2", "sec_0", "sec_1")


EXACT = lax.Precision.HIGHEST


def cut_along(x, dim, length):
    before, after = (x.shape[:dim], x.shape[dim + 1 :])
    return jnp.moveaxis(x.reshape(*before, length, -1, *after), dim, 0)


def scatter_pairs(x, chips, core, dim):
    sizes = (lax.axis_size(chips), lax.axis_size(core))
    blocks = cut_along(x, dim, sizes[0] * sizes[1])
    inside = blocks.shape[1:]
    blocks = blocks.reshape(*sizes, *inside).swapaxes(0, 1).reshape(-1, *inside)
    blocks = lax.psum_scatter(blocks, core, scatter_dimension=0, tiled=True)
    return lax.psum_scatter(blocks, chips, scatter_dimension=0, tiled=True)[0]


def shifted(block, axis, distance):
    devices = range(lax.axis_size(axis))
    route = [((i - distance) % len(devices), i) for i in devices]
    return lax.ppermute(block, axis, route)


def over_axes(x, axes):
    for axis in axes:
        x = lax.psum(x, axis)
    return x


def filled_up(lines, length):
    spare = -len(lines) % length
    return jnp.pad(lines, [(0, spare)] + [(0, 0)] * (lines.ndim - 1))


def sent_to_all(x, axis):
    length = lax.axis_size(axis)
    return lax.all_to_all(jnp.broadcast_to(x[None], (length, *x.shape)), axis, 0, 0, tiled=True)


def joined_along(blocks, dim):
    lengths = list(blocks.shape[1:])
    lengths[dim] *= blocks.shape[0]
    return jnp.moveaxis(blocks, 0, dim).reshape(lengths)


def whole_of(x, axes, dim):
    far, near = axes
    blocks = sent_to_all(sent_to_all(x, far), near)
    return joined_along(blocks.swapaxes(0, 1).reshape(-1, *x.shape), dim)


def sum_at_owner(x, axis, dim):
    length = lax.axis_size(axis)
    blocks = lax.all_to_all(cut_along(x, dim, length), axis, 0, 0, tiled=True)
    return jnp.sum(blocks, axis=0)


def summed_rows(x, axes, dim):
    far, near = axes
    own = sum_at_owner(cut_along(x, dim, lax.axis_size(far)), near, dim + 1)
    return jnp.sum(lax.all_to_all(own, far, 0, 0, tiled=True), axis=0)


def sum_by_parts(x, axes):
    lines = x.reshape(-1, x.shape[-1])
    padded = filled_up(lines, lax.axis_size(axes[0]) * lax.axis_size(axes[1]))
    whole = whole_of(summed_rows(padded, axes, 0), axes, 0)
    return lax.slice_in_dim(whole, 0, len(lines)).reshape(x.shape)


def matmul(first, second):
    return jnp.dot(first, second, precision=EXACT, preferred_element_type=jnp.float32)


def contract_rows(first, second):
    return jnp.einsum("rk,rl->kl", first, second, precision=EXACT)


def body(left_ops, right_ops, amplitudes, sketch, sector_shift):
    left_op = left_ops[0, 0]
    right_op = right_ops[0, 0]
    state_slab = amplitudes[0]
    offset = sector_shift[0]
    right_part = matmul(lax.all_gather(state_slab, OP, axis=0, tiled=True), right_op)
    term_full = matmul(left_op, right_part)
    slot_mask = (jnp.arange(4, dtype=jnp.int32) == offset)[:, None, None]
    stacked = jnp.where(slot_mask, term_full[None], jnp.zeros((), jnp.float32))
    class_parts = scatter_pairs(stacked, ("op_0", "op_1"), "op_2", 1)
    moved_one = shifted((class_parts[1], class_parts[3]), SEC, 1)
    moved_two = shifted(class_parts[2] + moved_one[1], SEC, 2)
    product_slab = class_parts[0] + moved_one[0] + moved_two
    correlation = jnp.sum(state_slab * product_slab)
    norm_sq = jnp.sum(state_slab * state_slab)
    totals = (over_axes(correlation, OP_SEC), over_axes(norm_sq, OP_SEC))
    energy = totals[0] / totals[1]
    residual = product_slab - energy * state_slab
    sketched = matmul(residual, sketch)
    gram_mat = sum_by_parts(contract_rows(sketched, sketched), (("op_0", "op_1"), "op_2"))
    factor = jnp.linalg.cholesky(gram_mat)
    basis_slab = jax.scipy.linalg.solve_triangular(factor, sketched.T, lower=True).T
    candidates = basis_slab[None]
    for bit_index in range(2):
        arrived = shifted(candidates, SEC, -(1 << bit_index))
        candidates = jnp.concatenate([candidates, arrived], axis=0)
    all_full = lax.all_gather(candidates, OP, axis=1, tiled=True)
    basis_full = all_full[0]
    target = lax.dynamic_index_in_dim(all_full, offset, 0, keepdims=False)
    applied = matmul(left_op, basis_full)
    rotated = contract_rows(target, applied)
    return (rotated[None, None], basis_slab[None], energy)


def solution(mesh):
    split = Mesh(mesh.devices.reshape(4, 4, 2, 4, 2), ("op_0", "op_1", "op_2", "sec_0", "sec_1"))
    in_specs = (P(OP, SEC, None, None), P(OP, SEC, None, None), P(SEC, OP, None), P(), P(OP))
    out_specs = (P(OP, SEC, None, None), P(SEC, OP, None), P())
    return jax.shard_map(body, mesh=split, in_specs=in_specs, out_specs=out_specs, check_vma=False)
```

profile of v0, /device:TPU:56, one launch (start us, length us, event | category | flops | bytes accessed | tf_op | source)
XLA Modules:
  0.0 653.3 jit_solution(6092954768310711771)
XLA Ops:
  8.6 63.7 %all-gather.6.cloned.1.call-done = f32[1,1024,1024]{2,1,0:T(8,128)} async-done(((f32[1,32,1024]{2,1,0:T(8,128)}), f32[1,1024,1024]{2,1,0:T(8,128)}) %all-gather.6.cloned.1.call-update) | async-done | bytes 4194320 | tf_op jit(solution)/shard_map/all_gather | solution.py:95
  72.3 17.3 %fusion.4 = f32[1024,1024]{1,0:T(8,128)S(1)} fusion(f32[1,1,1024,1024]{3,2,1,0:T(8,128)} %param.6, f32[1,1024,1024]{2,1,0:T(8,128)} %all-gather.6.cloned.1.call-done), kind=kOutput, calls=%fused_computation.7 | convolution fusion | flops 12884901888 | bytes 12582912 | tf_op jit(solution)/shard_map/dot_general | solution.py:83
  89.7 14.1 %fusion.2 = f32[1024,1024]{0,1:T(8,128)S(1)} fusion(f32[1024,1024]{1,0:T(8,128)S(1)} %fusion.4, f32[1,1,1024,1024]{3,2,1,0:T(8,128)S(1)} %copy-done.1), kind=kOutput, calls=%fused_computation.5 | convolution fusion | flops 12884901888 | bytes 12582912 | tf_op jit(solution)/shard_map/dot_general | solution.py:83
  104.3 8.0 %broadcast_select_fusion = f32[32,4,32,1024]{3,2,1,0:T(8,128)} fusion(f32[32,32,1024]{2,1,0:T(8,128)S(1)} %bitcast.125, pred[4]{0:T(512)(128)(4,1)S(1)} %iota_compare_fusion.3), kind=kLoop, calls=%fused_computation.2 | loop fusion | flops 4194304 | bytes 20971524 | tf_op jit(solution)/shard_map/jit(_where)/select_n | solution.py:98
  112.4 29.6 %reduce-scatter.3.cloned.1.call-done = f32[16,4,32,1024]{3,2,1,0:T(8,128)} async-done(((f32[32,4,32,1024]{3,2,1,0:T(8,128)}), f32[16,4,32,1024]{3,2,1,0:T(8,128)}) %reduce-scatter.3.cloned.1.call-update) | async-done | bytes 8388624 | tf_op jit(solution)/shard_map/reduce_scatter | solution.py:25
  142.0 126.2 %reduce-scatter.5.cloned.1.call-done = f32[1,4,32,1024]{3,2,1,0:T(8,128)} async-done(((f32[16,4,32,1024]{3,2,1,0:T(8,128)}), f32[1,4,32,1024]{3,2,1,0:T(8,128)}) %reduce-scatter.5.cloned.1.call-update) | async-done | bytes 524304 | tf_op jit(solution)/shard_map/reduce_scatter | solution.py:26
  271.2 3.8 collective-permute-done.1
  276.5 4.5 collective-permute-done.2
  282.6 11.1 %all-reduce.3 = (f32[]{:T(128)}, f32[]{:T(128)}) all-reduce(f32[]{:T(128)} %get-tuple-element.12, f32[]{:T(128)} %get-tuple-element.11), channel_id=1, replica_groups=mesh['op_0'=4,'op_1'=4,'op_2'=2,'sec_0'=4,'sec_1'=2] {'op_0'}, use_global_device_ids=true, to_apply=%region_3.4 | all-reduce | flops 2 | bytes 16 | tf_op jit(solution)/shard_map/psum | solution.py:37
  293.6 11.6 %all-reduce.2 = (f32[]{:T(128)}, f32[]{:T(128)}) all-reduce(f32[]{:T(128)} %get-tuple-element.25, f32[]{:T(128)} %get-tuple-element.26), channel_id=1, replica_groups=mesh['op_0'=4,'op_1'=4,'op_2'=2,'sec_0'=4,'sec_1'=2] {'op_1'}, use_global_device_ids=true, to_apply=%region_4.5 | all-reduce | flops 2 | bytes 16 | tf_op jit(solution)/shard_map/psum | solution.py:37
  308.4 8.8 %all-reduce.1 = (f32[]{:T(128)}, f32[]{:T(128)}) all-reduce(f32[]{:T(128)} %get-tuple-element.29, f32[]{:T(128)} %get-tuple-element.30), channel_id=1, replica_groups=mesh['op_0'=4,'op_1'=4,'op_2'=2,'sec_0'=4,'sec_1'=2] {'sec_0'}, use_global_device_ids=true, to_apply=%region_6.7 | all-reduce | flops 2 | bytes 16 | tf_op jit(solution)/shard_map/psum | solution.py:37
  317.2 6.0 all-reduce.4
  327.9 4.6 all_to_all.20
  333.4 21.9 %all_to_all.21 = f32[16,16,512]{2,1,0:T(8,128)S(1)} all-to-all(f32[16,16,512]{2,1,0:T(8,128)} %reduce_sum.38), channel_id=1, replica_groups=mesh['op_0'=4,'op_1'=4,'op_2'=2,'sec_0'=4,'sec_1'=2] {'op_0','op_1'}, dimensions={0} | all-to-all | bytes 1048576 | tf_op jit(solution)/shard_map/all_to_all | solution.py:72
  356.2 4.4 all-to-all-start.2
  360.7 15.7 %all-to-all-done.2 = f32[16,16,512]{2,1,0:T(8,128)S(1)} async-done(((f32[16,16,512]{2,1,0:T(8,128)}), f32[16,16,512]{2,1,0:T(8,128)S(1)}, u32[]{:S(2)}, u32[]{:S(2)}) %all-to-all-start.2) | async-done | bytes 524320 | tf_op jit(solution)/shard_map/all_to_all | solution.py:48
  376.6 4.6 all_to_all.22
  384.9 11.7 %cholesky.104 = f32[128,128]{1,0:T(8,128)S(1)} custom-call(f32[128,128]{1,0:T(8,128)S(1)} %cholesky.266), custom_call_target="Cholesky" | custom-call | tf_op jit(solution)/shard_map/jit(cholesky)/cholesky | solution.py:110
  396.8 9.8 %custom-call.31 = f32[1,128,128]{1,2,0:T(8,128)S(1)} custom-call(f32[1,128,128]{2,1,0:T(8,128)S(1)} %get-tuple-element.44), custom_call_target="InvertDiagBlocksLowerTriangular" | custom-call | tf_op jit(solution)/shard_map/jit(cholesky)/cholesky | solution.py:110
  409.1 11.7 %cholesky.217 = f32[128,128]{1,0:T(8,128)S(1)} custom-call(f32[128,128]{1,0:T(8,128)S(1)} %cholesky.270), custom_call_target="Cholesky" | custom-call | tf_op jit(solution)/shard_map/jit(cholesky)/cholesky | solution.py:110
  420.9 10.0 %custom-call.32 = f32[1,128,128]{1,2,0:T(8,128)S(1)} custom-call(f32[1,128,128]{2,1,0:T(8,128)S(1)} %get-tuple-element.41), custom_call_target="InvertDiagBlocksLowerTriangular" | custom-call | tf_op jit(solution)/shard_map/jit(cholesky)/cholesky | solution.py:110
  432.4 11.7 %cholesky.238 = f32[128,128]{1,0:T(8,128)S(1)} custom-call(f32[128,128]{1,0:T(8,128)S(1)} %cholesky.275), custom_call_target="Cholesky" | custom-call | tf_op jit(solution)/shard_map/jit(cholesky)/cholesky | solution.py:110
  444.9 9.8 %custom-call.33 = f32[1,128,128]{1,2,0:T(8,128)S(1)} custom-call(f32[1,128,128]{2,1,0:T(8,128)S(1)} %get-tuple-element.38), custom_call_target="InvertDiagBlocksLowerTriangular" | custom-call | tf_op jit(solution)/shard_map/jit(cholesky)/cholesky | solution.py:110
  456.1 11.7 %cholesky.255 = f32[128,128]{1,0:T(8,128)S(1)} custom-call(f32[128,128]{1,0:T(8,128)S(1)} %convolution_subtract_fusion.2), custom_call_target="Cholesky" | custom-call | tf_op jit(solution)/shard_map/jit(cholesky)/cholesky | solution.py:110
  473.1 14.1 %while.1 = (s32[]{:T(128)}, f32[512,512]{1,0:T(8,128)}, s32[4,2]{0,1:T(2,128)S(1)}, f32[4,128,128]{2,1,0:T(8,128)}, s32[]{:T(128)}) while((s32[]{:T(128)}, f32[512,512]{1,0:T(8,128)}, s32[4,2]{0,1:T(2,128)S(1)}, f32[4,128,128]{2,1,0:T(8,128)}, s32[]{:T(128)}) %tuple.33), condition=%wide.while_cond, body=%wide.while_body.sunk | while | flops 2 | bytes 132705 | solution.py:111
  487.2 40.1 %custom-call.34 = f32[4,128,128]{1,2,0:T(8,128)S(1)} custom-call(f32[4,128,128]{2,1,0:T(8,128)} %get-tuple-element.10), custom_call_target="InvertDiagBlocksLowerTriangular" | custom-call | tf_op jit(solution)/shard_map/jit(_solve_triangular)/triangular_solve | solution.py:111
  531.5 4.4 collective-permute-start.3
  535.9 3.3 collective-permute-done.3
  539.8 5.7 collective-permute-done.4
  546.3 73.8 %all-gather.4.cloned.1.call-done = f32[4,1024,512]{2,1,0:T(8,128)} async-done(((f32[4,32,512]{2,1,0:T(8,128)}), f32[4,1024,512]{2,1,0:T(8,128)}) %all-gather.4.cloned.1.call-update) | async-done | bytes 8388624 | tf_op jit(solution)/shard_map/all_gather | solution.py:116
  620.1 16.0 %fusion = f32[512,1024]{1,0:T(8,128)S(1)} fusion(f32[1,1,1024,1024]{3,2,1,0:T(8,128)} %param.5, f32[4,1024,512]{2,1,0:T(8,128)} %all-gather.4.cloned.1.call-done), kind=kOutput, calls=%fused_computation.3 | convolution fusion | flops 6442450944 | bytes 8388608 | tf_op jit(solution)/shard_map/dot_general | solution.py:83
  636.1 9.3 %fusion.10 = f32[1,1,512,512]{3,2,1,0:T(8,128)} fusion(f32[512,1024]{1,0:T(8,128)S(1)} %fusion, f32[4,1024,512]{2,1,0:T(8,128)} %all-gather.4.cloned.1.call-done, s32[]{:T(128)S(6)} %select_n.19), kind=kOutput, calls=%fused_computation.14 | convolution fusion | flops 3221225472 | bytes 5242884 | tf_op jit(solution)/shard_map/rk,rl->kl/dot_general | solution.py:87
  (82 shorter events, 48.3 us)
Async XLA Ops:
  7.2 317.4 %copy-start = (f32[1024,512]{1,0:T(8,128)S(1)}, f32[1024,512]{1,0:T(8,128)}, u32[]{:S(2)}) copy-start(f32[1024,512]{1,0:T(8,128)} %param.8) | copy-start | bytes 6291460
  7.2 65.2 %all-gather.6.cloned.1.call-start = ((), (), s32[]{:S(2)}) async-start(), calls=%async_computation.9 | async-start | bytes 4325376 | tf_op jit(solution)/shard_map/all_gather | solution.py:95
  7.9 134.1 %reduce-scatter.3.cloned.1.call-start = ((), (), s32[]{:S(2)}) async-start(), calls=%async_computation.6 | async-start | bytes 25165824 | tf_op jit(solution)/shard_map/reduce_scatter | solution.py:25
  72.3 17.3 %copy-start.1 = (f32[1,1,1024,1024]{3,2,1,0:T(8,128)S(1)}, f32[1,1,1024,1024]{3,2,1,0:T(8,128)}, u32[]{:S(2)}) copy-start(f32[1,1,1024,1024]{3,2,1,0:T(8,128)} %param.5) | copy-start | bytes 12582916
  112.3 155.9 %reduce-scatter.5.cloned.1.call-start = ((), (), s32[]{:S(2)}) async-start(), calls=%async_computation.7 | async-start | bytes 8912896 | tf_op jit(solution)/shard_map/reduce_scatter | solution.py:26
  142.0 139.0 %copy-start.3 = (f32[1,32,1024]{2,1,0:T(8,128)S(1)}, f32[1,32,1024]{2,1,0:T(8,128)}, u32[]{:S(2)}) copy-start(f32[1,32,1024]{2,1,0:T(8,128)} %param.7) | copy-start | bytes 393220
  269.2 5.8 collective-permute-start.1
  270.0 6.5 %collective-permute-start = (f32[32,1024]{1,0:T(8,128)S(1)}, f32[32,1024]{1,0:T(8,128)S(1)}, u32[]{:S(2)}, u32[]{:S(2)}) collective-permute-start(f32[32,1024]{1,0:T(8,128)S(1)} %get-tuple-element.33), channel_id=1, source_target_pairs={{7,0},{0,1},{1,2},{2,3},{3,4},{4,5},{5,6},{6,7},{15,8},{8,9},{9,10... | collective-permute-start | bytes 393224 | tf_op jit(solution)/shard_map/ppermute | solution.py:32
  276.0 5.0 collective-permute-start.2
  356.2 20.2 %all-to-all-start.2 = ((f32[16,16,512]{2,1,0:T(8,128)}), f32[16,16,512]{2,1,0:T(8,128)S(1)}, u32[]{:S(2)}, u32[]{:S(2)}) async-start(f32[16,16,512]{2,1,0:T(8,128)} %broadcast_in_dim.55), calls=%async_computation.4 | async-start | bytes 1048576 | tf_op jit(solution)/shard_map/all_to_all | solution.py:48
  360.7 259.4 %all-gather.4.cloned.1.call-start = ((), (), s32[]{:S(2)}) async-start(), calls=%async_computation.8 | async-start | bytes 8650752 | tf_op jit(solution)/shard_map/all_gather | solution.py:116
  383.9 1.0 copy-start.2
  531.5 104.6 %copy-start.4 = (f32[1,32,512]{2,1,0:T(8,128)}, f32[1,32,512]{2,1,0:T(8,128)S(1)}, u32[]{:S(2)}) copy-start(f32[1,32,512]{2,1,0:T(8,128)S(1)} %maximum_bitcast_fusion) | copy-start | bytes 196612
  531.5 7.7 %collective-permute-start.3 = (f32[1,32,512]{2,1,0:T(8,128)S(1)}, f32[1,32,512]{2,1,0:T(8,128)S(1)}, u32[]{:S(2)}, u32[]{:S(2)}) collective-permute-start(f32[1,32,512]{2,1,0:T(8,128)S(1)} %maximum_bitcast_fusion), channel_id=1, source_target_pairs={{1,0},{2,1},{3,2},{4,3},{5,4},{6,5},{7,6},{0,7},{9,8},{10,9},{11,1... | collective-permute-start | bytes 196616 | tf_op jit(solution)/shard_map/ppermute | solution.py:32
  539.2 6.3 collective-permute-start.4
Sparse Core Ops, SparseCore 0:
  10.5 61.7 all-gather.5
  112.5 29.5 reduce-scatter.2
  145.7 122.4 reduce-scatter.4
  546.4 73.6 all-gather.3
where the time goes:
time: 660 us; the launch traced here: 653 us
  waiting for transfers between devices  327 us (50%)
  other arithmetic  134 us (20%)
  blocking collectives  71.8 us (11%)
  matrix products  69.6 us (11%)
  between operations  19.9 us (3%)
  local copies, waits for them, and re-layouts  19.1 us (3%)
  starting transfers between devices  12.1 us (2%)
    reduce_scatter x1, waiting for transfers between devices, scatter_pairs(): return lax.psum_scatter(blocks, chips, scatter_dimension=0, tiled=True)[0]  126 us
    another operation x14, other arithmetic, body(): factor = jnp.linalg.cholesky(gram_mat)  78.6 us
    all_gather x1, waiting for transfers between devices, body(): all_full = lax.all_gather(candidates, OP, axis=1, tiled=True)  73.8 us
    all_gather x1, waiting for transfers between devices, body(): lax.all_gather(state_slab, OP, axis=0, tiled=True)  63.7 us
    dot_general x4, matrix products, matmul(): jnp.dot(first, second, precision=EXACT, preferred_element_type=jnp.float32)  49.7 us
    another operation x3, other arithmetic, body(): jax.scipy.linalg.solve_triangular(factor, sketched.T, lower=True)  41.6 us
    psum x5, blocking collectives, over_axes(): x = lax.psum(x, axis)  40.7 us
    reduce_scatter x1, waiting for transfers between devices, scatter_pairs(): blocks = lax.psum_scatter(blocks, core, scatter_dimension=0, tiled=True)  29.6 us
  transfers between devices with their start and end apart: 10, of which 9 were waited for; matrix products, arithmetic and copies ran while one was open for 0% of the time, Pallas kernels for 0%

commit v1 on v0

v1 whole, which is shorter than its diff:
```python
import jax
import jax.numpy as jnp
from jax import lax
from jax.experimental import pallas as pl
from jax.experimental.pallas import tpu as pltpu
from jax.sharding import Mesh
from jax.sharding import PartitionSpec as P

OP = ("op_0", "op_1", "op_2")
SEC = ("sec_0", "sec_1")
OP_SEC = ("op_0", "op_1", "op_2", "sec_0", "sec_1")
CLASSES = 4
NB = 128
STEP = 8
EXACT = lax.Precision.HIGHEST
CLOSE = lax.Precision.HIGH


def dot(first, second, dims, precision=EXACT):
    return lax.dot_general(first, second, (dims, ((), ())), precision=precision, preferred_element_type=jnp.float32)


def matmul(first, second, precision=EXACT):
    return dot(first, second, ((1,), (0,)), precision)


def contract_rows(first, second, precision=EXACT):
    return dot(first, second, ((0,), (0,)), precision)


def contract_cols(first, second, precision=EXACT):
    return dot(first, second, ((1,), (1,)), precision)


def unit_factor(block, step):
    sub = lax.broadcasted_iota(jnp.int32, (8, NB), 0)
    lane = lax.broadcasted_iota(jnp.int32, (8, NB), 1)
    rows = [block[8 * r : 8 * r + 8] for r in range(NB // 8)]
    for start in range(0, NB, step):
        live = range(start // 8, NB // 8)
        cols = [{r: jnp.broadcast_to(rows[r][:, start + q : start + q + 1], (8, NB)) for r in live} for q in range(step)]
        for q in range(step):
            j = start + q
            at, inside = divmod(j, 8)
            one = slice(inside, inside + 1)
            inv = 1.0 / cols[q][at][one]
            line = jnp.broadcast_to(jnp.where(lane[:1] == j, 1.0, rows[at][one]) * inv, (8, NB))
            later = {p: jnp.broadcast_to(cols[p][at][one] * inv, (8, NB)) for p in range(q + 1, step)}
            for r in range(at, NB // 8):
                factor = cols[q][r]
                hit = lane == j
                if r == at:
                    factor = jnp.where(sub > inside, factor, 0.0)
                    hit = hit & (sub > inside)
                rows[r] = jnp.where(hit, 0.0, rows[r]) - factor * line
                for p in later:
                    cols[p][r] = cols[p][r] - factor * later[p]
    return jnp.concatenate(rows, axis=0)


def inverse_factor_kernel(gram, out, work, low):
    n = gram.shape[0]
    work[...] = gram[...]
    low[...] = jnp.zeros_like(low)
    out[...] = jnp.zeros_like(out)
    row = lax.broadcasted_iota(jnp.int32, (NB, NB), 0)
    col = lax.broadcasted_iota(jnp.int32, (NB, NB), 1)

    def panel(p, carried):
        at = pl.ds(pl.multiple_of(p * NB, NB), NB)
        done = unit_factor(work[at, at], STEP)
        pivots = jnp.sum(jnp.where(row == col, done, 0.0), axis=1, keepdims=True)
        unit = jnp.where(row > col, done, jnp.where(row == col, 1.0, 0.0))
        inv = unit * (1.0 / jnp.sqrt(pivots))
        below = lax.broadcasted_iota(jnp.int32, (n, NB), 0) >= (p + 1) * NB
        panel_col = jnp.where(below, contract_cols(work[:, at], inv), 0.0)
        work[...] = work[...] - contract_cols(panel_col, panel_col)
        out[at, :] = -matmul(inv, matmul(low[at, :], out[...]))
        out[at, at] = inv
        low[:, at] = panel_col
        return carried

    lax.fori_loop(0, n // NB, panel, 0)


def inverse_factor(gram):
    in_vmem = pl.BlockSpec(memory_space=pltpu.VMEM)
    return pl.pallas_call(
        inverse_factor_kernel,
        out_shape=jax.ShapeDtypeStruct(gram.shape, jnp.float32),
        in_specs=[in_vmem],
        out_specs=in_vmem,
        scratch_shapes=[pltpu.VMEM(gram.shape, jnp.float32)] * 2,
        name="inverse_factor",
    )(gram)


def class_sums_kernel(shifts, blocks, out):
    k = pl.program_id(0)

    @pl.when(k == 0)
    def _():
        out[...] = jnp.zeros_like(out)

    for i in range(blocks.shape[0]):
        c = shifts[k * blocks.shape[0] + i]
        out[c] = out[c] + blocks[i]


def class_sums(blocks, shifts):
    count, rows, width = blocks.shape
    per = 4
    return pl.pallas_call(
        class_sums_kernel,
        out_shape=jax.ShapeDtypeStruct((CLASSES, rows, width), jnp.float32),
        grid=(count // per,),
        in_specs=[pl.BlockSpec(memory_space=pltpu.SMEM), pl.BlockSpec((per, rows, width), lambda k: (k, 0, 0))],
        out_specs=pl.BlockSpec((CLASSES, rows, width), lambda k: (0, 0, 0)),
        name="class_sums",
    )(shifts, blocks)


def shifted(block, axis, distance):
    length = lax.axis_size(axis)
    return lax.ppermute(block, axis, [((i - distance) % length, i) for i in range(length)])


def sent_to_all(x, axis):
    length = lax.axis_size(axis)
    return lax.all_to_all(jnp.broadcast_to(x[None], (length, *x.shape)), axis, 0, 0, tiled=True)


def stacked_over(x, axis, dim):
    length = lax.axis_size(axis)
    here = lax.axis_index(axis)
    arrived = [x] + [shifted(x, axis, d) for d in range(1, length)]
    whole = jnp.zeros((*x.shape[:dim], length, *x.shape[dim:]), x.dtype)
    for d in range(length):
        whole = lax.dynamic_update_index_in_dim(whole, arrived[d], (here - d) % length, dim)
    return whole


def gathered_rows(x):
    whole = stacked_over(stacked_over(stacked_over(x, "op_1", 0), "op_0", 0), "op_2", 2)
    return whole.reshape(-1, x.shape[-1])


TRI = [(i, j) for i in range(4) for j in range(i + 1)]


def packed(low):
    return jnp.stack([low[i * NB : i * NB + NB, j * NB : j * NB + NB] for i, j in TRI])


def unpacked(blocks):
    blank = jnp.zeros((NB, NB), jnp.float32)
    rows = [[blocks[TRI.index((i, j))] if j <= i else blank for j in range(4)] for i in range(4)]
    return jnp.concatenate([jnp.concatenate(r, axis=1) for r in rows], axis=0)


def from_target(x, offset):
    for bit in range(2):
        arrived = shifted(x, SEC, -(1 << bit))
        x = jnp.where((offset >> bit) % 2 == 1, arrived, x)
    return x


def body(left_ops, right_ops, amplitudes, sketch, sector_shift):
    left_op = left_ops[0, 0]
    right_op = right_ops[0, 0]
    state_slab = amplitudes[0]
    offset = sector_shift[0]
    shifts = sent_to_all(jnp.broadcast_to(sector_shift.astype(jnp.float32)[:, None], (1, 128)), OP)[:, 0, 0].astype(jnp.int32)
    term = matmul(left_op, matmul(gathered_rows(state_slab), right_op))
    blocks = lax.all_to_all(term.reshape(32, -1, term.shape[-1]), OP, 0, 0, tiled=True)
    class_parts = class_sums(blocks, shifts)
    product_slab = class_parts[0] + shifted(class_parts[1], SEC, 1) + shifted(class_parts[2], SEC, 2) + shifted(class_parts[3], SEC, 3)
    partial = jnp.stack([jnp.sum(state_slab * product_slab), jnp.sum(state_slab * state_slab)])
    totals = jnp.sum(sent_to_all(jnp.pad(partial, (0, 126))[None], OP_SEC), axis=(0, 1))
    energy = totals[0] / totals[1]
    sketched = matmul(product_slab - energy * state_slab, sketch)
    candidates = sketched[None]
    for bit in range(2):
        candidates = jnp.concatenate([candidates, shifted(candidates, SEC, -(1 << bit))], axis=0)
    all_full = lax.all_gather(candidates, OP, axis=1, tiled=True)
    own_full = gathered_rows(sketched)
    inverse = inverse_factor(contract_rows(own_full, own_full))
    basis_slab = contract_cols(sketched, inverse)
    target_inverse = unpacked(from_target(packed(inverse), offset))
    applied = matmul(left_op, contract_cols(own_full, inverse, CLOSE), CLOSE)
    target = lax.dynamic_index_in_dim(all_full, offset, 0, keepdims=False)
    rotated = matmul(target_inverse, contract_rows(target, applied, CLOSE), CLOSE)
    return (rotated[None, None], basis_slab[None], energy)


def solution(mesh):
    split = Mesh(mesh.devices.reshape(4, 4, 2, 4, 2), ("op_0", "op_1", "op_2", "sec_0", "sec_1"))
    in_specs = (P(OP, SEC, None, None), P(OP, SEC, None, None), P(SEC, OP, None), P(), P(OP))
    out_specs = (P(OP, SEC, None, None), P(SEC, OP, None), P())
    return jax.shard_map(body, mesh=split, in_specs=in_specs, out_specs=out_specs, check_vma=False)
```

time: 660 us -> 397 us (0.60)
  waiting for transfers between devices: 327 us -> 167 us
  other arithmetic: 134 us -> 6.13 us
  blocking collectives: 71.8 us -> 21.8 us
  starting transfers between devices: 12.1 us -> 60.1 us
  Pallas kernels: 0 us -> 31.1 us
  matrix products: 69.6 us -> 56 us
  local copies, waits for them, and re-layouts: 19.1 us -> 31.5 us
    reduce_scatter x2 -> x0, waiting for transfers between devices: 156 us -> none  [the longest x1 126 us: scatter_pairs(): return lax.psum_scatter(blocks, chips, scatter_dimension=0, tiled=True)[0]]
    another operation x17 -> x1, other arithmetic: 120 us -> 1.37 us  [body(): jnp.stack([jnp.sum(state_slab * product_slab), jnp.sum(state_slab * state...]
    all_to_all x0 -> x1, waiting for transfers between devices: none -> 85.7 us  [body(): lax.all_to_all(term.reshape(32, -1, term.shape[-1]), OP, 0, 0, tiled=True)]
    all_gather x1, waiting for transfers between devices: 73.8 us -> 0.02 us  [body(): all_full = lax.all_gather(candidates, OP, axis=1, tiled=True)]
    ppermute x5 -> x21, waiting for transfers between devices: 17.3 us -> 81.3 us  [shifted(): lax.ppermute(block, axis, [((i - distance) % length, i) for i in range(le...]
    all_gather x1 -> x0, waiting for transfers between devices: 63.7 us -> none  [body(): lax.all_gather(state_slab, OP, axis=0, tiled=True)]
    psum x5 -> x0, blocking collectives: 40.7 us -> none  [over_axes(): x = lax.psum(x, axis)]
    ppermute x5 -> x21, starting transfers between devices: 7.55 us -> 42.4 us  [shifted(): lax.ppermute(block, axis, [((i - distance) % length, i) for i in range(le...]
  transfers between devices with their start and end apart: 10 -> 24, of which waited for: 9 -> 18; matrix products, arithmetic and copies ran while one was open for 0% -> 19% of each run, Pallas kernels for 0% -> 7%
where the time goes in v1:
time: 397 us; the launch traced here: 391 us
  waiting for transfers between devices  167 us (42%)
  starting transfers between devices  60.1 us (15%)
  matrix products  56 us (14%)
  local copies, waits for them, and re-layouts  31.5 us (8%)
  Pallas kernels  31.1 us (8%)
  blocking collectives  21.8 us (5%)
  between operations  17.8 us (4%)
  other arithmetic  6.13 us (2%)
    all_to_all x1, waiting for transfers between devices, body(): lax.all_to_all(term.reshape(32, -1, term.shape[-1]), OP, 0, 0, tiled=True)  85.7 us
    ppermute x21, waiting for transfers between devices, shifted(): lax.ppermute(block, axis, [((i - distance) % length, i) for i in range(le...  81.3 us
    dot_general x9, matrix products, dot(): lax.dot_general(first, second, (dims, ((), ())), precision=precision, pre...  56 us
    ppermute x21, starting transfers between devices, shifted(): lax.ppermute(block, axis, [((i - distance) % length, i) for i in range(le...  42.4 us
    pallas_call x1, Pallas kernels, inverse_factor(): pl.pallas_call(inverse_factor_kernel, out_shape=jax.ShapeDtypeStruct(gram...  25.6 us
    all_to_all x1, blocking collectives, sent_to_all(): lax.all_to_all(jnp.broadcast_to(x[None], (length, *x.shape)), axis, 0, 0,...  21.8 us
    unnamed x23, local copies, waits for them, and re-layouts  15.6 us
    all_to_all x1, starting transfers between devices, body(): lax.all_to_all(term.reshape(32, -1, term.shape[-1]), OP, 0, 0, tiled=True)  10 us
  transfers between devices with their start and end apart: 24, of which 18 were waited for; matrix products, arithmetic and copies ran while one was open for 19% of the time, Pallas kernels for 7%

profile of v1, /device:TPU:56, one launch (start us, length us, event | category | flops | bytes accessed | tf_op | source)
XLA Modules:
  0.0 391.5 jit_solution(18416798415509287274)
XLA Ops:
  7.2 3.3 collective-permute-start
  10.5 4.5 %collective-permute-start.1 = (f32[32,1024]{1,0:T(8,128)}, f32[32,1024]{1,0:T(8,128)S(1)}, u32[]{:S(2)}, u32[]{:S(2)}) collective-permute-start(f32[32,1024]{1,0:T(8,128)} %bitcast.177), channel_id=1, source_target_pairs={{32,0},{48,16},{0,32},{16,48},{33,1},{49,17},{1,33},{17,49},{34,2}... | collective-permute-start | bytes 393224 | tf_op jit(solution)/shard_map/ppermute | solution.py:125
  15.0 2.7 collective-permute-start.2
  19.9 2.5 collective-permute-done.1
  22.4 2.7 collective-permute-done.2
  26.7 2.7 collective-permute-start.4
  33.3 7.1 %collective-permute-done.3 = f32[4,32,1024]{2,1,0:T(8,128)} collective-permute-done((f32[4,32,1024]{2,1,0:T(8,128)S(1)}, f32[4,32,1024]{2,1,0:T(8,128)}, u32[]{:S(2)}, u32[]{:S(2)}) %collective-permute-start.3) | collective-permute-done | bytes 524320 | tf_op jit(solution)/shard_map/ppermute | solution.py:125
  42.2 8.9 %collective-permute-done.4 = f32[4,32,1024]{2,1,0:T(8,128)S(1)} collective-permute-done((f32[4,32,1024]{2,1,0:T(8,128)S(1)}, f32[4,32,1024]{2,1,0:T(8,128)S(1)}, u32[]{:S(2)}, u32[]{:S(2)}) %collective-permute-start.4) | collective-permute-done | bytes 524320 | tf_op jit(solution)/shard_map/ppermute | solution.py:125
  54.0 7.7 %all-to-all-start = ((f32[32,1,128]{2,1,0:T(1,128)}), f32[32,1,128]{2,1,0:T(1,128)S(1)}, u32[]{:S(2)}, u32[]{:S(2)}) async-start(f32[32,1,128]{2,1,0:T(1,128)} %broadcast_in_dim_broadcast_in_dim_broadcast_in_dim.8), calls=%async_computation | async-start | bytes 32768 | tf_op jit(solution)/shard_map/all_to_all | solution.py:130
  66.9 13.4 %fusion.4 = f32[1024,1024]{1,0:T(8,128)S(1)} fusion(f32[1024,1024]{1,0:T(8,128)S(1)} %bitcast.175, f32[1,1,1024,1024]{3,2,1,0:T(8,128)S(1)} %copy-done.6), kind=kOutput, calls=%fused_computation.4 | convolution fusion | flops 12884901888 | bytes 12582912 | tf_op jit(solution)/shard_map/dot_general | solution.py:20
  80.4 15.4 %fusion.2 = f32[1024,1024]{0,1:T(8,128)} fusion(f32[1024,1024]{1,0:T(8,128)S(1)} %fusion.4, f32[1,1,1024,1024]{3,2,1,0:T(8,128)S(1)} %copy-done.3), kind=kOutput, calls=%fused_computation.2 | convolution fusion | flops 12884901888 | bytes 12582912 | tf_op jit(solution)/shard_map/dot_general | solution.py:20
  95.8 10.0 %all-to-all-start.1 = ((f32[32,32,1024]{2,1,0:T(8,128)}), f32[32,32,1024]{2,1,0:T(8,128)}, u32[]{:S(2)}, u32[]{:S(2)}) async-start(f32[32,32,1024]{2,1,0:T(8,128)} %bitcast.174), calls=%async_computation.1 | async-start | bytes 8388608 | tf_op jit(solution)/shard_map/all_to_all | solution.py:175
  107.1 85.7 %all-to-all-done.1.blocks = f32[32,32,1024]{2,1,0:T(8,128)} async-done(((f32[32,32,1024]{2,1,0:T(8,128)}), f32[32,32,1024]{2,1,0:T(8,128)}, u32[]{:S(2)}, u32[]{:S(2)}) %all-to-all-start.1) | async-done | bytes 4194336 | tf_op jit(solution)/shard_map/all_to_all | solution.py:175
  192.8 5.6 %class_sums.1 = f32[4,32,1024]{2,1,0:T(8,128)} custom-call(s32[32]{0:T(128)} %fusion.51.shifts, f32[32,32,1024]{2,1,0:T(8,128)} %all-to-all-done.1.blocks), custom_call_target="tpu_custom_call" | custom-call | tf_op jit(solution)/shard_map/class_sums/pallas_call | solution.py:113
  199.5 13.8 %collective-permute-start.9 = (f32[32,1024]{1,0:T(8,128)S(1)}, f32[32,1024]{1,0:T(8,128)S(1)}, u32[]{:S(2)}, u32[]{:S(2)}) collective-permute-start(f32[32,1024]{1,0:T(8,128)S(1)} %get-tuple-element.17), channel_id=1, source_target_pairs={{5,0},{6,1},{7,2},{0,3},{1,4},{2,5},{3,6},{4,7},{13,8},{14,9},{15,... | collective-permute-start | bytes 393224 | tf_op jit(solution)/shard_map/ppermute | solution.py:125
  213.3 2.2 collective-permute-start.8
  223.4 21.8 %all_to_all.15 = f32[256,1,128]{2,1,0:T(1,128)S(1)} all-to-all(f32[256,1,128]{2,1,0:T(1,128)S(1)} %broadcast_in_dim.113), channel_id=1, replica_groups=mesh['op_0'=4,'op_1'=4,'op_2'=2,'sec_0'=4,'sec_1'=2] {'op_0','op_1','op_..., dimensions={0} | all-to-all | bytes 262144 | tf_op jit(solution)/shard_map/all_to_all | solution.py:130
  249.6 5.4 %collective-permute-done.19 = f32[1,32,512]{2,1,0:T(8,128)S(1)} collective-permute-done((f32[1,32,512]{2,1,0:T(8,128)S(1)}, f32[1,32,512]{2,1,0:T(8,128)S(1)}, u32[]{:S(2)}, u32[]{:S(2)}) %collective-permute-start.19) | collective-permute-done | bytes 65568 | tf_op jit(solution)/shard_map/ppermute | solution.py:125
  255.0 6.2 %collective-permute-done.20 = f32[2,32,512]{2,1,0:T(8,128)S(1)} collective-permute-done((f32[2,32,512]{2,1,0:T(8,128)S(1)}, f32[2,32,512]{2,1,0:T(8,128)S(1)}, u32[]{:S(2)}, u32[]{:S(2)}) %collective-permute-start.20) | collective-permute-done | bytes 131104 | tf_op jit(solution)/shard_map/ppermute | solution.py:125
  262.8 2.5 collective-permute-start.11
  266.9 2.1 collective-permute-done.10
  269.1 3.3 collective-permute-done.11
  276.5 11.5 %collective-permute-done.13 = f32[4,32,512]{2,1,0:T(8,128)S(1)} collective-permute-done((f32[4,32,512]{2,1,0:T(8,128)S(1)}, f32[4,32,512]{2,1,0:T(8,128)S(1)}, u32[]{:S(2)}, u32[]{:S(2)}) %collective-permute-start.13) | collective-permute-done | bytes 262176 | tf_op jit(solution)/shard_map/ppermute | solution.py:125
  288.8 2.3 collective-permute-done.16
  292.6 4.6 %convolution_bitcast_fusion.1.gram = f32[512,512]{1,0:T(8,128)} fusion(f32[4,4,2,32,512]{4,3,2,1,0:T(8,128)S(1)} %bitcast_dynamic-update-slice_fusion.3), kind=kOutput, calls=%fused_computation.12 | convolution fusion | flops 3221225472 | bytes 3145728 | tf_op jit(solution)/shard_map/dot_general | solution.py:20
  297.2 25.6 %inverse_factor.1 = f32[512,512]{1,0:T(8,128)} custom-call(f32[512,512]{1,0:T(8,128)} %convolution_bitcast_fusion.1.gram), custom_call_target="tpu_custom_call" | custom-call | tf_op jit(solution)/shard_map/inverse_factor/pallas_call | solution.py:88
  337.6 19.2 %collective-permute-done.17 = f32[10,128,128]{2,1,0:T(8,128)} collective-permute-done((f32[10,128,128]{2,1,0:T(8,128)}, f32[10,128,128]{2,1,0:T(8,128)}, u32[]{:S(2)}, u32[]{:S(2)}) %collective-permute-start.17) | collective-permute-done | bytes 655392 | tf_op jit(solution)/shard_map/ppermute | solution.py:125
  358.3 3.6 fusion.60
  363.6 8.2 %fusion = f32[512,1024]{1,0:T(8,128)} fusion(f32[1024,512]{1,0:T(8,128)S(1)} %fusion.60, f32[1,1,1024,1024]{3,2,1,0:T(8,128)S(1)} %copy-done.4), kind=kOutput, calls=%fused_computation | convolution fusion | flops 3221225472 | bytes 8388608 | tf_op jit(solution)/shard_map/dot_general | solution.py:20
  371.8 3.5 collective-permute-done.18
  375.5 5.7 %fusion.6 = f32[512,512]{1,0:T(8,128)S(1)} fusion(f32[512,1024]{1,0:T(8,128)} %fusion, f32[4,1024,512]{2,1,0:T(8,128)} %all-gather.2.cloned.1.call-done, s32[]{:T(128)S(6)} %select_n.161), kind=kOutput, calls=%fused_computation.7 | convolution fusion | flops 1610612736 | bytes 5242884 | tf_op jit(solution)/shard_map/dot_general | solution.py:20
  381.3 2.0 convolution_bitcast_fusion
  (93 shorter events, 58.0 us)
Async XLA Ops:
  7.2 240.0 %copy-start = (f32[1024,512]{1,0:T(8,128)S(1)}, f32[1024,512]{1,0:T(8,128)}, u32[]{:S(2)}) copy-start(f32[1024,512]{1,0:T(8,128)} %param.8) | copy-start | bytes 6291460
  7.2 12.7 %collective-permute-start = (f32[32,1024]{1,0:T(8,128)}, f32[32,1024]{1,0:T(8,128)S(1)}, u32[]{:S(2)}, u32[]{:S(2)}) collective-permute-start(f32[32,1024]{1,0:T(8,128)} %bitcast.176), channel_id=1, source_target_pairs={{48,0},{0,16},{16,32},{32,48},{49,1},{1,17},{17,33},{33,49},{50,2}... | collective-permute-start | bytes 393224 | tf_op jit(solution)/shard_map/ppermute | solution.py:125
  10.5 11.8 %collective-permute-start.1 = (f32[32,1024]{1,0:T(8,128)}, f32[32,1024]{1,0:T(8,128)S(1)}, u32[]{:S(2)}, u32[]{:S(2)}) collective-permute-start(f32[32,1024]{1,0:T(8,128)} %bitcast.177), channel_id=1, source_target_pairs={{32,0},{48,16},{0,32},{16,48},{33,1},{49,17},{1,33},{17,49},{34,2}... | collective-permute-start | bytes 393224 | tf_op jit(solution)/shard_map/ppermute | solution.py:125
  15.0 10.1 %collective-permute-start.2 = (f32[32,1024]{1,0:T(8,128)}, f32[32,1024]{1,0:T(8,128)S(1)}, u32[]{:S(2)}, u32[]{:S(2)}) collective-permute-start(f32[32,1024]{1,0:T(8,128)} %bitcast.178), channel_id=1, source_target_pairs={{16,0},{32,16},{48,32},{0,48},{17,1},{33,17},{49,33},{1,49},{18,2}... | collective-permute-start | bytes 393224 | tf_op jit(solution)/shard_map/ppermute | solution.py:125
  25.1 15.2 %collective-permute-start.3 = (f32[4,32,1024]{2,1,0:T(8,128)S(1)}, f32[4,32,1024]{2,1,0:T(8,128)}, u32[]{:S(2)}, u32[]{:S(2)}) collective-permute-start(f32[4,32,1024]{2,1,0:T(8,128)S(1)} %bitcast_dynamic-update-slice_fusion.12), channel_id=1, source_target_pairs={{192,0},{0,64},{64,128},{128,192},{193,1},{1,65},{65,129},{129,193... | collective-permute-start | bytes 1572872 | tf_op jit(solution)/shard_map/ppermute | solution.py:125
  26.7 24.4 %collective-permute-start.4 = (f32[4,32,1024]{2,1,0:T(8,128)S(1)}, f32[4,32,1024]{2,1,0:T(8,128)S(1)}, u32[]{:S(2)}, u32[]{:S(2)}) collective-permute-start(f32[4,32,1024]{2,1,0:T(8,128)S(1)} %bitcast_dynamic-update-slice_fusion.12), channel_id=1, source_target_pairs={{128,0},{192,64},{0,128},{64,192},{129,1},{193,65},{1,129},{65,193... | collective-permute-start | bytes 1572872 | tf_op jit(solution)/shard_map/ppermute | solution.py:125
  29.4 22.5 %collective-permute-start.5 = (f32[4,32,1024]{2,1,0:T(8,128)S(1)}, f32[4,32,1024]{2,1,0:T(8,128)S(1)}, u32[]{:S(2)}, u32[]{:S(2)}) collective-permute-start(f32[4,32,1024]{2,1,0:T(8,128)S(1)} %bitcast_dynamic-update-slice_fusion.12), channel_id=1, source_target_pairs={{64,0},{128,64},{192,128},{0,192},{65,1},{129,65},{193,129},{1,193... | collective-permute-start | bytes 1572872 | tf_op jit(solution)/shard_map/ppermute | solution.py:125
  52.8 11.4 %collective-permute-start.6 = (f32[4,4,32,1024]{3,2,1,0:T(8,128)}, f32[4,4,32,1024]{3,2,1,0:T(8,128)}, u32[]{:S(2)}, u32[]{:S(2)}) collective-permute-start(f32[4,4,32,1024]{3,2,1,0:T(8,128)} %bitcast_dynamic-update-slice_fusion.4), channel_id=1, source_target_pairs={{8,0},{0,8},{9,1},{1,9},{10,2},{2,10},{11,3},{3,11},{12,4},{4,12},... | collective-permute-start | bytes 6291464 | tf_op jit(solution)/shard_map/ppermute | solution.py:125
  54.0 41.8 %all-to-all-start = ((f32[32,1,128]{2,1,0:T(1,128)}), f32[32,1,128]{2,1,0:T(1,128)S(1)}, u32[]{:S(2)}, u32[]{:S(2)}) async-start(f32[32,1,128]{2,1,0:T(1,128)} %broadcast_in_dim_broadcast_in_dim_broadcast_in_dim.8), calls=%async_computation | async-start | bytes 32768 | tf_op jit(solution)/shard_map/all_to_all | solution.py:130
  64.1 2.8 copy-start.6
  66.9 13.4 %copy-start.3 = (f32[1,1,1024,1024]{3,2,1,0:T(8,128)S(1)}, f32[1,1,1024,1024]{3,2,1,0:T(8,128)}, u32[]{:S(2)}) copy-start(f32[1,1,1024,1024]{3,2,1,0:T(8,128)} %param.5) | copy-start | bytes 12582916
  95.8 97.0 %all-to-all-start.1 = ((f32[32,32,1024]{2,1,0:T(8,128)}), f32[32,32,1024]{2,1,0:T(8,128)}, u32[]{:S(2)}, u32[]{:S(2)}) async-start(f32[32,32,1024]{2,1,0:T(8,128)} %bitcast.174), calls=%async_computation.1 | async-start | bytes 8388608 | tf_op jit(solution)/shard_map/all_to_all | solution.py:175
  105.9 269.7 %all-gather.2.cloned.1.call-start = ((), (), s32[]{:S(2)}) async-start(), calls=%async_computation.3 | async-start | bytes 8650752 | tf_op jit(solution)/shard_map/all_gather | solution.py:185
  107.1 113.3 %copy-start.5 = (f32[1,32,1024]{2,1,0:T(8,128)S(1)}, f32[1,32,1024]{2,1,0:T(8,128)}, u32[]{:S(2)}) copy-start(f32[1,32,1024]{2,1,0:T(8,128)} %param.7) | copy-start | bytes 393220
  199.5 17.4 %collective-permute-start.9 = (f32[32,1024]{1,0:T(8,128)S(1)}, f32[32,1024]{1,0:T(8,128)S(1)}, u32[]{:S(2)}, u32[]{:S(2)}) collective-permute-start(f32[32,1024]{1,0:T(8,128)S(1)} %get-tuple-element.17), channel_id=1, source_target_pairs={{5,0},{6,1},{7,2},{0,3},{1,4},{2,5},{3,6},{4,7},{13,8},{14,9},{15,... | collective-permute-start | bytes 393224 | tf_op jit(solution)/shard_map/ppermute | solution.py:125
  213.3 5.3 %collective-permute-start.8 = (f32[32,1024]{1,0:T(8,128)S(1)}, f32[32,1024]{1,0:T(8,128)S(1)}, u32[]{:S(2)}, u32[]{:S(2)}) collective-permute-start(f32[32,1024]{1,0:T(8,128)S(1)} %get-tuple-element.18), channel_id=1, source_target_pairs={{6,0},{7,1},{0,2},{1,3},{2,4},{3,5},{4,6},{5,7},{14,8},{15,9},{8,1... | collective-permute-start | bytes 393224 | tf_op jit(solution)/shard_map/ppermute | solution.py:125
  215.4 5.0 %collective-permute-start.7 = (f32[32,1024]{1,0:T(8,128)S(1)}, f32[32,1024]{1,0:T(8,128)S(1)}, u32[]{:S(2)}, u32[]{:S(2)}) collective-permute-start(f32[32,1024]{1,0:T(8,128)S(1)} %get-tuple-element.16), channel_id=1, source_target_pairs={{7,0},{0,1},{1,2},{2,3},{3,4},{4,5},{5,6},{6,7},{15,8},{8,9},{9,10... | collective-permute-start | bytes 393224 | tf_op jit(solution)/shard_map/ppermute | solution.py:125
  248.5 6.5 %collective-permute-start.19 = (f32[1,32,512]{2,1,0:T(8,128)S(1)}, f32[1,32,512]{2,1,0:T(8,128)S(1)}, u32[]{:S(2)}, u32[]{:S(2)}) collective-permute-start(f32[1,32,512]{2,1,0:T(8,128)S(1)} %bitcast.179), channel_id=1, source_target_pairs={{1,0},{2,1},{3,2},{4,3},{5,4},{6,5},{7,6},{0,7},{9,8},{10,9},{11,1... | collective-permute-start | bytes 196616 | tf_op jit(solution)/shard_map/ppermute | solution.py:125
  255.0 6.3 %collective-permute-start.20 = (f32[2,32,512]{2,1,0:T(8,128)S(1)}, f32[2,32,512]{2,1,0:T(8,128)S(1)}, u32[]{:S(2)}, u32[]{:S(2)}) collective-permute-start(f32[2,32,512]{2,1,0:T(8,128)S(1)} %pad_maximum_fusion.1), channel_id=1, source_target_pairs={{2,0},{3,1},{4,2},{5,3},{6,4},{7,5},{0,6},{1,7},{10,8},{11,9},{12,... | collective-permute-start | bytes 393224 | tf_op jit(solution)/shard_map/ppermute | solution.py:125
  262.0 7.1 %collective-permute-start.10 = (f32[32,512]{1,0:T(8,128)S(1)}, f32[32,512]{1,0:T(8,128)S(1)}, u32[]{:S(2)}, u32[]{:S(2)}) collective-permute-start(f32[32,512]{1,0:T(8,128)S(1)} %get-tuple-element.22), channel_id=1, source_target_pairs={{48,0},{0,16},{16,32},{32,48},{49,1},{1,17},{17,33},{33,49},{50,2}... | collective-permute-start | bytes 196616 | tf_op jit(solution)/shard_map/ppermute | solution.py:125
  262.8 9.6 %collective-permute-start.11 = (f32[32,512]{1,0:T(8,128)S(1)}, f32[32,512]{1,0:T(8,128)S(1)}, u32[]{:S(2)}, u32[]{:S(2)}) collective-permute-start(f32[32,512]{1,0:T(8,128)S(1)} %get-tuple-element.22), channel_id=1, source_target_pairs={{32,0},{48,16},{0,32},{16,48},{33,1},{49,17},{1,33},{17,49},{34,2}... | collective-permute-start | bytes 196616 | tf_op jit(solution)/shard_map/ppermute | solution.py:125
  265.4 7.5 %collective-permute-start.12 = (f32[32,512]{1,0:T(8,128)S(1)}, f32[32,512]{1,0:T(8,128)S(1)}, u32[]{:S(2)}, u32[]{:S(2)}) collective-permute-start(f32[32,512]{1,0:T(8,128)S(1)} %get-tuple-element.22), channel_id=1, source_target_pairs={{16,0},{32,16},{48,32},{0,48},{17,1},{33,17},{49,33},{1,49},{18,2}... | collective-permute-start | bytes 196616 | tf_op jit(solution)/shard_map/ppermute | solution.py:125
  272.9 15.1 %collective-permute-start.13 = (f32[4,32,512]{2,1,0:T(8,128)S(1)}, f32[4,32,512]{2,1,0:T(8,128)S(1)}, u32[]{:S(2)}, u32[]{:S(2)}) collective-permute-start(f32[4,32,512]{2,1,0:T(8,128)S(1)} %bitcast_dynamic-update-slice_fusion.15), channel_id=1, source_target_pairs={{192,0},{0,64},{64,128},{128,192},{193,1},{1,65},{65,129},{129,193... | collective-permute-start | bytes 786440 | tf_op jit(solution)/shard_map/ppermute | solution.py:125
  273.6 14.5 %collective-permute-start.14 = (f32[4,32,512]{2,1,0:T(8,128)S(1)}, f32[4,32,512]{2,1,0:T(8,128)S(1)}, u32[]{:S(2)}, u32[]{:S(2)}) collective-permute-start(f32[4,32,512]{2,1,0:T(8,128)S(1)} %bitcast_dynamic-update-slice_fusion.15), channel_id=1, source_target_pairs={{128,0},{192,64},{0,128},{64,192},{129,1},{193,65},{1,129},{65,193... | collective-permute-start | bytes 786440 | tf_op jit(solution)/shard_map/ppermute | solution.py:125
  275.6 12.5 %collective-permute-start.15 = (f32[4,32,512]{2,1,0:T(8,128)S(1)}, f32[4,32,512]{2,1,0:T(8,128)S(1)}, u32[]{:S(2)}, u32[]{:S(2)}) collective-permute-start(f32[4,32,512]{2,1,0:T(8,128)S(1)} %bitcast_dynamic-update-slice_fusion.15), channel_id=1, source_target_pairs={{64,0},{128,64},{192,128},{0,192},{65,1},{129,65},{193,129},{1,193... | collective-permute-start | bytes 786440 | tf_op jit(solution)/shard_map/ppermute | solution.py:125
  288.1 2.9 collective-permute-start.16
  291.2 1.4 copy-start.2
  322.8 35.5 %copy-start.1 = (f32[512,512]{1,0:T(8,128)S(1)}, f32[512,512]{1,0:T(8,128)}, u32[]{:S(2)}) copy-start(f32[512,512]{1,0:T(8,128)} %inverse_factor.1) | copy-start | bytes 3145732
  337.6 19.2 %collective-permute-start.17 = (f32[10,128,128]{2,1,0:T(8,128)}, f32[10,128,128]{2,1,0:T(8,128)}, u32[]{:S(2)}, u32[]{:S(2)}) collective-permute-start(f32[10,128,128]{2,1,0:T(8,128)} %fusion.40), channel_id=1, source_target_pairs={{1,0},{2,1},{3,2},{4,3},{5,4},{6,5},{7,6},{0,7},{9,8},{10,9},{11,1... | collective-permute-start | bytes 1966088 | tf_op jit(solution)/shard_map/ppermute | solution.py:125
  358.0 17.4 %collective-permute-start.18 = (f32[10,128,128]{2,1,0:T(8,128)S(1)}, f32[10,128,128]{2,1,0:T(8,128)S(1)}, u32[]{:S(2)}, u32[]{:S(2)}) collective-permute-start(f32[10,128,128]{2,1,0:T(8,128)S(1)} %broadcast_select_fusion), channel_id=1, source_target_pairs={{2,0},{3,1},{4,2},{5,3},{6,4},{7,5},{0,6},{1,7},{10,8},{11,9},{12,... | collective-permute-start | bytes 1966088 | tf_op jit(solution)/shard_map/ppermute | solution.py:125
  358.3 5.3 %copy-start.4 = (f32[1,1,1024,1024]{3,2,1,0:T(8,128)S(1)}, f32[1,1,1024,1024]{3,2,1,0:T(8,128)}, u32[]{:S(2)}) copy-start(f32[1,1,1024,1024]{3,2,1,0:T(8,128)} %param.5) | copy-start | bytes 12582916
Sparse Core Ops, SparseCore 0:
  262.1 74.2 all-gather.1
